TPU v7x, 256 devices: a whole 4x4x8 slice. The times are simulated.
256 devices in a mesh: band: 32 (over y_lo, z, core), fft: 8 (over y_hi, x).
Axes of the slice: x: 4, y: 4 (y_hi: 2, y_lo: 2; y = y_hi * 2 + y_lo), z: 8, core: 2. Of those that a mesh axis runs over, the one named last changes fastest.
Arguments:
- orbitals: float32 [64, 128, 128, 128], P('band', 'fft'), may hold values from -6 to 6
- owners: int32 [1], replicated, may hold values from 0 to 31
- local_pick: int32 [32, 1], P('band'), may hold values from 0 to 1
Outputs:
- exchange_term: float32 [32, 128, 128, 128], P('band', 'fft')
All inputs are finite; a program needn't handle non-finite values.
Results may differ from a plain program's by a relative error of at most 0.0003.
Values sent between devices are 32-bit elements; how exact they have to be, the bound alone decides.
A program may use at most 64 MiB of HBM per device.

v0:
```python
import math

import jax
import jax.numpy as jnp
from jax import lax
from jax.sharding import PartitionSpec as P

NG = 128


def spread(shard, axis, root):
    mine = lax.axis_index(axis) == root
    return lax.psum(jnp.where(mine, shard, jnp.zeros_like(shard)), axis)


def dft_tables(size):
    index = jnp.arange(size, dtype=jnp.int32)
    product = index[:, None] * index[None, :] % size
    angle = product.astype(jnp.float32) * (2.0 * math.pi / size)
    return (jnp.cos(angle), jnp.sin(angle))


def signed_freq(index, size):
    return jnp.where(index < size // 2, index, index - size).astype(jnp.float32)


def along(form, data, table):
    return jnp.einsum(form, data, table, precision=lax.Precision.HIGHEST)


def transform(density, cosine, sine, kernel):
    last_form = "pzxy,yk->pzxk"
    middle_form = "pzxy,xk->pzky"
    first_form = "pzab,zk->pkab"
    real_part = along(last_form, density, cosine)
    imag_part = -along(last_form, density, sine)
    mixed_real = along(middle_form, real_part, cosine) + along(middle_form, imag_part, sine)
    mixed_imag = along(middle_form, imag_part, cosine) - along(middle_form, real_part, sine)
    line_real = lax.all_to_all(mixed_real, "fft", split_axis=2, concat_axis=1, tiled=True)
    line_imag = lax.all_to_all(mixed_imag, "fft", split_axis=2, concat_axis=1, tiled=True)
    spec_real = along(first_form, line_real, cosine) + along(first_form, line_imag, sine)
    spec_imag = along(first_form, line_imag, cosine) - along(first_form, line_real, sine)
    spec_real = spec_real * kernel
    spec_imag = spec_imag * kernel
    back_real = along(first_form, spec_real, cosine) - along(first_form, spec_imag, sine)
    back_imag = along(first_form, spec_imag, cosine) + along(first_form, spec_real, sine)
    slab_real = lax.all_to_all(back_real, "fft", split_axis=1, concat_axis=2, tiled=True)
    slab_imag = lax.all_to_all(back_imag, "fft", split_axis=1, concat_axis=2, tiled=True)
    inner_real = along(middle_form, slab_real, cosine) - along(middle_form, slab_imag, sine)
    inner_imag = along(middle_form, slab_imag, cosine) + along(middle_form, slab_real, sine)
    first_field = along(last_form, inner_real, cosine) - along(last_form, inner_imag, sine)
    return first_field


def on_device(orbitals, owners, local_pick):
    cosine, sine = dft_tables(NG)
    groups = lax.axis_size("fft")
    width = NG // groups
    start = lax.axis_index("fft") * width
    freq_first = signed_freq(jnp.arange(NG, dtype=jnp.int32), NG)
    freq_second = signed_freq(start + jnp.arange(width, dtype=jnp.int32), NG)
    square = (
        freq_first[:, None, None] ** 2
        + freq_second[None, :, None] ** 2
        + freq_first[None, None, :] ** 2
    )
    scale = 0.25 * NG * math.sqrt(NG) / (NG * NG * NG)
    kernel = jnp.where(square > 0, scale / jnp.maximum(square, 1.0), 0.0)
    selected = jnp.take(orbitals, local_pick[0], axis=0)
    count_local = selected.shape[0]
    grid_shape = selected.shape[1:]
    sent_all = spread(orbitals, "band", owners[0])
    potentials = transform(
        (sent_all[:, None] * selected[None]).reshape(
            (sent_all.shape[0] * count_local,) + grid_shape
        ),
        cosine,
        sine,
        kernel,
    )
    shaped = potentials.reshape((sent_all.shape[0], count_local) + grid_shape)
    return jnp.sum(shaped * sent_all[:, None], axis=0)


def solution(mesh):
    in_specs = (P("band", "fft", None, None), P(), P("band", None))
    out_specs = P("band", "fft", None, None)
    return jax.shard_map(
        on_device, mesh=mesh, in_specs=in_specs, out_specs=out_specs, check_vma=False
    )
```

profile of v0, /device:TPU:1, one launch (start us, length us, event | category | flops | bytes accessed | tf_op | source)
XLA Modules:
  0.0 430.8 jit_solution(1754355146462454194)
XLA Ops:
  7.2 1.5 broadcast_select_fusion
  8.7 0.0 all-reduce.2.cloned.1.call-update
  9.6 0.8 copy-done.5
  10.3 0.1 fusion.34
  10.4 233.2 %all-reduce.2.cloned.1.call-done = f32[2,16,128,128]{3,2,1,0:T(8,128)} async-done(((f32[2,16,128,128]{3,2,1,0:T(8,128)}), f32[2,16,128,128]{3,2,1,0:T(8,128)}) %all-reduce.2.cloned.1.call-update) | async-done | bytes 2097168 | tf_op jit(solution)/shard_map/psum | solution.py:13
  243.6 3.7 fusion.20
  247.4 2.2 fusion.61
  249.6 0.2 copy-done.2
  249.7 2.1 fusion.18
  251.8 2.1 add_bitcast_fusion.1
  253.9 2.6 copy.58
  256.5 6.4 %all-to-all-start = ((f32[2,16,128,128]{3,1,0,2:T(8,128)}), f32[2,16,128,128]{3,1,0,2:T(8,128)}, u32[]{:S(2)}, u32[]{:S(2)}) async-start(f32[2,16,128,128]{3,1,0,2:T(8,128)} %copy.58), calls=%async_computation | async-start | bytes 4194304 | tf_op jit(solution)/shard_map/all_to_all | solution.py:39
  262.8 3.7 fusion.47
  266.6 2.1 subtract_bitcast_fusion.1
  268.7 2.5 copy.63
  271.2 20.3 %all-to-all-done = f32[2,16,128,128]{3,1,0,2:T(8,128)} async-done(((f32[2,16,128,128]{3,1,0,2:T(8,128)}), f32[2,16,128,128]{3,1,0,2:T(8,128)}, u32[]{:S(2)}, u32[]{:S(2)}) %all-to-all-start) | async-done | bytes 2097184 | tf_op jit(solution)/shard_map/all_to_all | solution.py:39
  291.5 6.3 %all-to-all-start.1 = ((f32[2,16,128,128]{3,1,0,2:T(8,128)}), f32[2,16,128,128]{3,1,0,2:T(8,128)}, u32[]{:S(2)}, u32[]{:S(2)}) async-start(f32[2,16,128,128]{3,1,0,2:T(8,128)} %copy.63), calls=%async_computation.1 | async-start | bytes 4194304 | tf_op jit(solution)/shard_map/all_to_all | solution.py:40
  297.8 0.1 broadcast_add_fusion
  297.9 0.3 fusion.33
  298.2 1.9 copy.59
  300.1 26.4 %all-to-all-done.1 = f32[2,16,128,128]{3,1,0,2:T(8,128)} async-done(((f32[2,16,128,128]{3,1,0,2:T(8,128)}), f32[2,16,128,128]{3,1,0,2:T(8,128)}, u32[]{:S(2)}, u32[]{:S(2)}) %all-to-all-start.1) | async-done | bytes 2097184 | tf_op jit(solution)/shard_map/all_to_all | solution.py:40
  326.5 1.9 copy.64
  328.4 2.2 fusion.58
  330.6 2.2 fusion.63
  332.7 2.5 subtract_multiply_fusion
  335.2 2.5 add_multiply_fusion
  337.7 0.0 copy-done
  337.7 2.2 fusion.4
  339.9 2.6 add_bitcast_fusion
  342.4 2.6 copy.76
  345.0 4.3 %all-to-all-start.3 = ((f32[2,128,16,128]{3,2,0,1:T(8,128)}), f32[2,128,16,128]{3,2,0,1:T(8,128)}, u32[]{:S(2)}, u32[]{:S(2)}) async-start(f32[2,128,16,128]{3,2,0,1:T(8,128)} %copy.76), calls=%async_computation.3 | async-start | bytes 4194304 | tf_op jit(solution)/shard_map/all_to_all | solution.py:48
  349.4 3.7 fusion.6
  353.1 2.2 subtract_bitcast_fusion
  355.3 2.5 copy.70
  357.8 20.1 %all-to-all-done.3 = f32[2,128,16,128]{3,2,0,1:T(8,128)} async-done(((f32[2,128,16,128]{3,2,0,1:T(8,128)}), f32[2,128,16,128]{3,2,0,1:T(8,128)}, u32[]{:S(2)}, u32[]{:S(2)}) %all-to-all-start.3) | async-done | bytes 2097184 | tf_op jit(solution)/shard_map/all_to_all | solution.py:48
  378.0 5.6 %all-to-all-start.2 = ((f32[2,128,16,128]{3,2,0,1:T(8,128)}), f32[2,128,16,128]{3,2,0,1:T(8,128)}, u32[]{:S(2)}, u32[]{:S(2)}) async-start(f32[2,128,16,128]{3,2,0,1:T(8,128)} %copy.70), calls=%async_computation.2 | async-start | bytes 4194304 | tf_op jit(solution)/shard_map/all_to_all | solution.py:47
  383.6 1.8 copy.78
  385.4 2.2 fusion.55
  387.6 3.5 fusion.43
  391.1 21.1 %all-to-all-done.2 = f32[2,128,16,128]{3,2,0,1:T(8,128)} async-done(((f32[2,128,16,128]{3,2,0,1:T(8,128)}), f32[2,128,16,128]{3,2,0,1:T(8,128)}, u32[]{:S(2)}, u32[]{:S(2)}) %all-to-all-start.2) | async-done | bytes 2097184 | tf_op jit(solution)/shard_map/all_to_all | solution.py:47
  412.2 1.8 copy.72
  414.0 2.2 fusion.40
  416.2 2.2 fusion.66
  418.4 0.0 copy-start.3
  418.4 0.0 copy-start.4
  418.4 2.1 fusion
  420.5 0.1 copy-done.4
  420.6 3.2 multiply_reduce_fusion
  (9 shorter events, 0.0 us)
Async XLA Ops:
  6.5 237.1 %all-reduce.2.cloned.1.call-start = ((), (), s32[]{:S(2)}) async-start(), calls=%async_computation.4 | async-start | bytes 4194304 | tf_op jit(solution)/shard_map/psum | solution.py:13
  8.7 1.6 copy-start.5
  247.3 4.4 %copy-start.1 = (f32[2,16,128,128]{3,2,1,0:T(8,128)}, f32[2,16,128,128]{3,2,1,0:T(8,128)S(1)}, u32[]{:S(2)}) copy-start(f32[2,16,128,128]{3,2,1,0:T(8,128)S(1)} %fusion.20) | copy-start | bytes 6291460
  247.4 2.3 copy-start.2
  256.5 35.1 %all-to-all-start = ((f32[2,16,128,128]{3,1,0,2:T(8,128)}), f32[2,16,128,128]{3,1,0,2:T(8,128)}, u32[]{:S(2)}, u32[]{:S(2)}) async-start(f32[2,16,128,128]{3,1,0,2:T(8,128)} %copy.58), calls=%async_computation | async-start | bytes 4194304 | tf_op jit(solution)/shard_map/all_to_all | solution.py:39
  291.5 35.0 %all-to-all-start.1 = ((f32[2,16,128,128]{3,1,0,2:T(8,128)}), f32[2,16,128,128]{3,1,0,2:T(8,128)}, u32[]{:S(2)}, u32[]{:S(2)}) async-start(f32[2,16,128,128]{3,1,0,2:T(8,128)} %copy.63), calls=%async_computation.1 | async-start | bytes 4194304 | tf_op jit(solution)/shard_map/all_to_all | solution.py:40
  335.2 2.5 copy-start
  345.0 33.0 %all-to-all-start.3 = ((f32[2,128,16,128]{3,2,0,1:T(8,128)}), f32[2,128,16,128]{3,2,0,1:T(8,128)}, u32[]{:S(2)}, u32[]{:S(2)}) async-start(f32[2,128,16,128]{3,2,0,1:T(8,128)} %copy.76), calls=%async_computation.3 | async-start | bytes 4194304 | tf_op jit(solution)/shard_map/all_to_all | solution.py:48
  378.0 34.2 %all-to-all-start.2 = ((f32[2,128,16,128]{3,2,0,1:T(8,128)}), f32[2,128,16,128]{3,2,0,1:T(8,128)}, u32[]{:S(2)}, u32[]{:S(2)}) async-start(f32[2,128,16,128]{3,2,0,1:T(8,128)} %copy.70), calls=%async_computation.2 | async-start | bytes 4194304 | tf_op jit(solution)/shard_map/all_to_all | solution.py:47
  418.4 2.1 copy-start.3
  418.4 2.2 copy-start.4
Sparse Core Ops, SparseCore 0:
  10.0 233.6 all-reduce.1
where the time goes:
time: 439 us; the launch traced here: 431 us
  waiting for transfers between devices  321 us (73%)
  matrix products  51.2 us (12%)
  starting transfers between devices  22.6 us (5%)
  local copies, waits for them, and re-layouts  18.6 us (4%)
  between operations  15.3 us (3%)
    psum x1, waiting for transfers between devices, spread(): return lax.psum(jnp.where(mine, shard, jnp.zeros_like(shard)), axis)  233 us
    dot_general x20, matrix products, along(): return jnp.einsum(form, data, table, precision=lax.Precision.HIGHEST)  51.2 us
    all_to_all x1, waiting for transfers between devices, transform(): lax.all_to_all(mixed_imag, 'fft', split_axis=2, concat_axis=1, tiled=True)  26.4 us
    all_to_all x1, waiting for transfers between devices, transform(): lax.all_to_all(back_real, 'fft', split_axis=1, concat_axis=2, tiled=True)  21.1 us
    all_to_all x1, waiting for transfers between devices, transform(): lax.all_to_all(mixed_real, 'fft', split_axis=2, concat_axis=1, tiled=True)  20.3 us
    all_to_all x1, waiting for transfers between devices, transform(): lax.all_to_all(back_imag, 'fft', split_axis=1, concat_axis=2, tiled=True)  20.1 us
  transfers between devices with their start and end apart: 5, of which 5 were waited for; matrix products, arithmetic and copies ran while one was open for 6% of the time, Pallas kernels for 0%

commit v1 on v0

v1 whole, which is shorter than its diff:
```python
import functools
import math

import jax
import jax.numpy as jnp
import numpy as np
from jax import lax
from jax.experimental import pallas as pl
from jax.experimental.pallas import tpu as pltpu
from jax.sharding import PartitionSpec as P

NG = 128
NZ = 8
NX = 4
FFT = 8
WIDE = NG // FFT
MESH = pl.DeviceIdType.MESH
SCALE = 0.25 * NG * math.sqrt(NG) / (NG * NG * NG)
ORDER = (1, 3, 4, 2, 5, 7, 6)


def tables():
    index = np.arange(NG)
    angle = (index[:, None] * index[None, :] % NG) * (2.0 * np.pi / NG)
    cosine, sine = np.cos(angle), np.sin(angle)
    right = np.block([[cosine, -sine], [sine, cosine]])
    out = []
    for table in (right, right.T):
        high = table.astype(jnp.bfloat16)
        low = (table - high.astype(np.float64)).astype(jnp.bfloat16)
        out += [high, low]
    return out


def split(value):
    high = value.astype(jnp.bfloat16)
    low = (value - high.astype(jnp.float32)).astype(jnp.bfloat16)
    return high, low


def dot(a, b):
    return jnp.dot(a, b, preferred_element_type=jnp.float32)


def on_right(value, high, low):
    vh, vl = split(value)
    return dot(vh, high) + (dot(vl, high) + dot(vh, low))


def on_left(high, low, value):
    vh, vl = split(value)
    return dot(high, vh) + (dot(high, vl) + dot(low, vh))


def stack(parts):
    return jnp.concatenate([jnp.concatenate(p, axis=0) for p in parts], axis=1)


def unstack(value):
    return jnp.concatenate(
        [
            jnp.concatenate([value[:NG, s], value[NG:, s]], axis=1)
            for s in (slice(0, NG), slice(NG, 2 * NG))
        ],
        axis=0,
    )


CHUNKS = 32
ROWS = WIDE * NG // CHUNKS


def spread_kernel(owner, x_ref, o_ref, ring_recv, pair_recv, ring_send, pair_send, root_send):
    y0, z0, c0 = owner // 16, owner // 2 % NZ, owner % 2
    band = lax.axis_index("band")
    y, z, c = band // 16, lax.rem(band // 2, NZ), lax.rem(band, 2)
    up, down = lax.rem(z + 1, NZ), lax.rem(z + NZ - 1, NZ)

    def at(yy, zz, cc):
        return {"band": yy * 16 + zz * 2 + cc}

    barrier = pltpu.get_barrier_semaphore()
    greet = [at(y, zz, cc) for zz in (up, down) for cc in (0, 1)]
    greet += [at(1 - y, z, cc) for cc in (0, 1)] + [at(y, z, 1 - c)]
    for device in greet:
        pl.semaphore_signal(barrier, inc=1, device_id=device, device_id_type=MESH)
    pl.semaphore_wait(barrier, len(greet))

    ahead = lax.rem(z - z0 + NZ, NZ)
    home = y == y0
    at_root = jnp.logical_and(home, ahead == 0)
    is_owner = jnp.logical_and(at_root, c == c0)
    goes_up = ahead < 4
    goes_down = jnp.logical_or(ahead == 0, ahead > 5)

    def piece(ref, orbital, i):
        return ref.at[orbital, pl.ds(i * ROWS, ROWS)]

    def send(src, orbital, i, send_sem, recv_sem, device):
        return pltpu.make_async_remote_copy(
            piece(src, orbital, i),
            piece(o_ref, orbital, i),
            send_sem,
            recv_sem,
            device_id=device,
            device_id_type=MESH,
        )

    @pl.when(is_owner)
    def _():
        def step(i, carry):
            for j in (0, 1):
                for kind, device in enumerate((at(y0, up, j), at(y0, down, j), at(1 - y0, z, j))):
                    send(x_ref, j, i, root_send.at[kind, j], ring_recv.at[i], device).start()
            return carry

        lax.fori_loop(0, CHUNKS, step, 0)
        whole = pltpu.make_async_remote_copy(
            x_ref, o_ref, pair_send.at[0], pair_recv, device_id=at(y0, z0, 1 - c0), device_id_type=MESH
        )
        whole.start()
        local = pltpu.make_async_copy(x_ref, o_ref, pair_send.at[1])
        local.start()
        for kind in range(3):
            for j in (0, 1):
                pltpu.make_async_copy(x_ref.at[0], x_ref.at[0], root_send.at[kind, j]).wait()
        whole.wait_send()
        local.wait()

    @pl.when(jnp.logical_and(at_root, c != c0))
    def _():
        pltpu.make_async_copy(x_ref, o_ref, pair_recv).wait()

    @pl.when(jnp.logical_not(at_root))
    def _():
        def step(i, carry):
            here = piece(o_ref, c, i)
            pltpu.make_async_copy(here, here, ring_recv.at[i]).wait()

            @pl.when(goes_up)
            def _():
                send(o_ref, c, i, ring_send.at[0], ring_recv.at[i], at(y, up, c)).start()

            @pl.when(goes_down)
            def _():
                send(o_ref, c, i, ring_send.at[1], ring_recv.at[i], at(y, down, c)).start()

            send(o_ref, c, i, pair_send.at[0], pair_recv, at(y, z, 1 - c)).start()
            return carry

        lax.fori_loop(0, CHUNKS, step, 0)
        block = o_ref.at[0]
        pltpu.make_async_copy(block, block, pair_send.at[0]).wait()

        @pl.when(goes_up)
        def _():
            pltpu.make_async_copy(block, block, ring_send.at[0]).wait()

        @pl.when(goes_down)
        def _():
            pltpu.make_async_copy(block, block, ring_send.at[1]).wait()

        pltpu.make_async_copy(block, block, pair_recv).wait()


def spread(owner, orbitals):
    vmem = pl.BlockSpec(memory_space=pltpu.VMEM)
    dma = pltpu.SemaphoreType.DMA
    flat = orbitals.reshape(2, WIDE * NG, NG)
    out = pl.pallas_call(
        functools.partial(spread_kernel, owner),
        out_shape=jax.ShapeDtypeStruct(flat.shape, flat.dtype),
        in_specs=[vmem],
        out_specs=vmem,
        scratch_shapes=[dma((CHUNKS,)), dma, dma((2,)), dma((2,)), dma((3, 2))],
        compiler_params=pltpu.CompilerParams(collective_id=1 + owner, has_side_effects=True),
        name=f"spread_{owner}",
    )(flat)
    return out.reshape(orbitals.shape)


def exchange(send_ref, recv_ref, start, count, send_sem, recv_sem, me):
    high, low = me // NX, lax.rem(me, NX)
    for k in ORDER:
        there = lax.rem(high + k // NX, 2) * NX + lax.rem(low + k % NX, NX)
        pltpu.make_async_remote_copy(
            send_ref.at[pl.ds(start, count), :, pl.ds(there * WIDE, WIDE)],
            recv_ref.at[pl.ds(me * WIDE + start, count)],
            send_sem.at[k],
            recv_sem.at[k],
            device_id={"fft": there},
            device_id_type=MESH,
        ).start()


def keep(send_ref, recv_ref, start, count, me):
    for i in range(count):
        recv_ref[me * WIDE + start + i] = send_ref[start + i, :, pl.ds(me * WIDE, WIDE)]


def arrived(recv_ref, recv_sem):
    block = recv_ref.at[pl.ds(0, WIDE)]
    for k in ORDER:
        pltpu.make_async_copy(block, block, recv_sem.at[k]).wait()


def lines(recv_ref, row):
    flat = recv_ref.reshape(NG * 2 * WIDE, NG)
    return [flat[pl.ds(part * WIDE + row, NG, stride=2 * WIDE), :] for part in (0, 1)]


def field_kernel(
    pick_ref, rh_ref, rl_ref, lh_ref, ll_ref, x_ref, s_ref, o_ref,
    send1, recv1, send2, recv2, ss1, rs1, ss2, rs2,
):
    me = lax.axis_index("fft")
    barrier = pltpu.get_barrier_semaphore()
    for k in range(1, FFT):
        pl.semaphore_signal(barrier, inc=1, device_id={"fft": lax.rem(me + k, FFT)}, device_id_type=MESH)
    pl.semaphore_wait(barrier, FFT - 1)
    pick = pick_ref[0, 0]

    def forward(i, carry):
        start = 2 * i
        rows = []
        for p in (0, 1):
            chosen = x_ref[pick, start + p]
            rows.append(jnp.concatenate([s_ref[0, start + p] * chosen, s_ref[1, start + p] * chosen], axis=1))
        value = on_right(jnp.concatenate(rows, axis=0), rh_ref[...], rl_ref[...])
        value = stack([[value[p * NG:(p + 1) * NG, :NG], value[p * NG:(p + 1) * NG, NG:]] for p in (0, 1)])
        value = on_left(lh_ref[...], ll_ref[...], value)
        for p in (0, 1):
            for part in (0, 1):
                send1[start + p, part] = value[part * NG:(part + 1) * NG, p * NG:(p + 1) * NG]
        exchange(send1, recv1, start, 2, ss1, rs1, me)
        keep(send1, recv1, start, 2, me)
        return carry

    lax.fori_loop(0, WIDE // 2, forward, 0)
    arrived(recv1, rs1)

    first = lax.broadcasted_iota(jnp.int32, (NG, NG), 0)
    last = lax.broadcasted_iota(jnp.int32, (NG, NG), 1)
    signed = lambda n: jnp.where(n < NG // 2, n, n - NG)
    first, last = signed(first), signed(last)
    plane = first * first + last * last

    def middle(i, carry):
        start = 2 * i
        value = stack([lines(recv1, start + p) for p in (0, 1)])
        value = on_left(lh_ref[...], ll_ref[...], value)
        filters = []
        for p in (0, 1):
            second = me * WIDE + start + p
            second = second - NG * (second // (NG // 2))
            square = plane + second * second
            ratio = SCALE / jnp.maximum(square, 1).astype(jnp.float32)
            filters.append(jnp.where(square > 0, ratio, 0.0))
        filters = jnp.concatenate(filters, axis=1)
        value = jnp.concatenate([value[:NG] * filters, value[NG:] * filters], axis=0)
        value = on_left(rh_ref[...], rl_ref[...], value)
        for p in (0, 1):
            for part in (0, 1):
                send2[start + p, part] = value[part * NG:(part + 1) * NG, p * NG:(p + 1) * NG]
        exchange(send2, recv2, start, 2, ss2, rs2, me)
        keep(send2, recv2, start, 2, me)
        return carry

    lax.fori_loop(0, WIDE // 2, middle, 0)
    arrived(recv2, rs2)

    def backward(i, carry):
        start = 2 * i
        value = stack([lines(recv2, start + p) for p in (0, 1)])
        value = on_left(rh_ref[...], rl_ref[...], value)
        value = on_right(unstack(value), lh_ref[...], ll_ref[...])
        for p in (0, 1):
            part = value[p * NG:(p + 1) * NG]
            o_ref[start + p] = part[:, :NG] * s_ref[0, start + p] + part[:, NG:] * s_ref[1, start + p]
        return carry

    lax.fori_loop(0, WIDE // 2, backward, 0)
    for sem, ref in ((ss1, recv1), (ss2, recv2)):
        arrived(ref, sem)


def field(pick, orbitals, sent):
    vmem = pl.BlockSpec(memory_space=pltpu.VMEM)
    dma = pltpu.SemaphoreType.DMA
    consts = [jnp.asarray(t) for t in tables()]
    return pl.pallas_call(
        field_kernel,
        out_shape=jax.ShapeDtypeStruct(orbitals.shape[1:], orbitals.dtype),
        in_specs=[pl.BlockSpec(memory_space=pltpu.SMEM)] + [vmem] * 6,
        out_specs=vmem,
        scratch_shapes=[
            pltpu.VMEM((WIDE, 2, NG, NG), jnp.float32),
            pltpu.VMEM((NG, 2, WIDE, NG), jnp.float32),
            pltpu.VMEM((WIDE, 2, NG, NG), jnp.float32),
            pltpu.VMEM((NG, 2, WIDE, NG), jnp.float32),
            dma((FFT,)), dma((FFT,)), dma((FFT,)), dma((FFT,)),
        ],
        compiler_params=pltpu.CompilerParams(collective_id=0, has_side_effects=True, vmem_limit_bytes=48 << 20),
        name="field",
    )(pick, *consts, orbitals, sent)


def on_device(orbitals, owners, local_pick):
    sent = lax.switch(owners[0], [functools.partial(spread, owner) for owner in range(32)], orbitals)
    return field(local_pick, orbitals, sent)[None]


def solution(mesh):
    in_specs = (P("band", "fft", None, None), P(), P("band", None))
    out_specs = P("band", "fft", None, None)
    return jax.shard_map(on_device, mesh=mesh, in_specs=in_specs, out_specs=out_specs, check_vma=False)
```

time: 439 us -> 134 us (0.31); the launches traced: 431 us -> 134 us
  waiting for transfers between devices: 321 us -> 0 us
  Pallas kernels: 0 us -> 131 us
  matrix products: 51.2 us -> 0 us
  starting transfers between devices: 22.6 us -> 0 us
  local copies, waits for them, and re-layouts: 18.6 us -> 1 us
  between operations: 15.3 us -> 1.38 us
    psum x1 -> x0, waiting for transfers between devices: 233 us -> none  [spread(): return lax.psum(jnp.where(mine, shard, jnp.zeros_like(shard)), axis)]
    pallas_call x0 -> x2, Pallas kernels: none -> 131 us  [the longest x1 66 us: field(): pl.pallas_call(field_kernel, out_shape=jax.ShapeDtypeStruct(orbitals.shap...]
    all_to_all x4 -> x0, waiting for transfers between devices: 87.9 us -> none  [the longest x1 26.4 us: transform(): lax.all_to_all(mixed_imag, 'fft', split_axis=2, concat_axis=1, tiled=True)]
    dot_general x20 -> x0, matrix products: 51.2 us -> none  [along(): return jnp.einsum(form, data, table, precision=lax.Precision.HIGHEST)]
    all_to_all x4 -> x0, starting transfers between devices: 22.6 us -> none  [the longest x1 6.36 us: transform(): lax.all_to_all(mixed_real, 'fft', split_axis=2, concat_axis=1, tiled=True)]
    all_to_all x4 -> x0, local copies, waits for them, and re-layouts: 7.35 us -> none  [the longest x1 1.86 us: transform(): lax.all_to_all(mixed_real, 'fft', split_axis=2, concat_axis=1, tiled=True)]
    add x2 -> x0, local copies, waits for them, and re-layouts: 5.12 us -> none  [the longest x1 2.56 us: transform(): along(middle_form, real_part, cosine) + along(middle_form, imag_part, sine)]
    sub x2 -> x0, local copies, waits for them, and re-layouts: 5.09 us -> none  [the longest x1 2.54 us: transform(): along(middle_form, imag_part, cosine) - along(middle_form, real_part, sine)]
  transfers between devices with their start and end apart: 5 -> 0, of which waited for: 5 -> 0; matrix products, arithmetic and copies ran while one was open for 6% -> 0% of each run, Pallas kernels for 0% -> 0%
where the time goes in v1:
time: 134 us
  Pallas kernels  131 us (98%)
  between operations  1.38 us (1%)
    pallas_call x1, Pallas kernels, field(): pl.pallas_call(field_kernel, out_shape=jax.ShapeDtypeStruct(orbitals.shap...  66 us
    pallas_call x1, Pallas kernels, spread(): pl.pallas_call(functools.partial(spread_kernel, owner), out_shape=jax.Sha...  65.1 us

profile of v1, /device:TPU:1, one launch (start us, length us, event | category | flops | bytes accessed | tf_op | source)
XLA Modules:
  0.0 133.5 jit_solution(2189616552240476471)
XLA Ops:
  0.7 0.0 copy-start
  0.7 0.0 copy-start.1
  0.7 0.0 copy-start.2
  0.7 0.0 copy-start.3
  0.7 65.1 %conditional.1 = (f32[2,16,128,128]{3,2,1,0:T(8,128)S(1)}) conditional(s32[]{:T(128)} %bitcast.64, f32[2,16,128,128]{3,2,1,0:T(8,128)} %x_ref.1, f32[2,16,128,128]{3,2,1,0:T(8,128)} %x_ref.1, f32[2,16,128,128]{3,2,1,0:T(8,128)} %x_ref.1, f32[2,16,128,128]{3,2,1,0:T(8,128)} %x_ref.1, ...), branch_computations={%region_0.0_spmd, %region_1.0_spmd, %region_2.0_spmd, %region_3.0_... | conditional | bytes 8 | solution.py:309
  0.8 65.1 %spread_23.1 = f32[2,2048,128]{2,1,0:T(8,128)S(1)} custom-call(f32[2,2048,128]{2,1,0:T(8,128)} %bitcast.90), custom_call_target="tpu_custom_call" | custom-call | tf_op jit(solution)/shard_map/cond/branch_23_fun/spread_23/pallas_call | solution.py:170
  66.5 0.0 copy-done
  66.5 0.0 copy-done.1
  66.5 0.0 copy-done.2
  66.5 0.0 copy-done.3
  66.5 66.0 %field.1 = f32[16,128,128]{2,1,0:T(8,128)S(1)} custom-call(s32[1,1]{1,0:T(1,128)S(6)} %copy.42.pick_ref, bf16[256,256]{1,0:T(8,128)(2,1)S(1)} %copy-done, bf16[256,256]{1,0:T(8,128)(2,1)S(1)} %copy-done.1, bf16[256,256]{1,0:T(8,128)(2,1)S(1)} %copy-done.2, bf16[256,256]{1,0:T(8,128)(2,1)S(1)} %copy-done.3, f32[2,16,128,128]{3,2,1,0:T(8,128)} %x_ref.1, ...), custom_call_target="tpu_custom_call" | custom-call | tf_op jit(solution)/shard_map/field/pallas_call | solution.py:291
  132.6 1.0 copy.43
Async XLA Ops:
  0.7 65.9 %copy-start = (bf16[256,256]{1,0:T(8,128)(2,1)S(1)}, bf16[256,256]{1,0:T(8,128)(2,1)}, u32[]{:S(2)}) copy-start(bf16[256,256]{1,0:T(8,128)(2,1)} %constant.14.clone.rh_ref) | copy-start | bytes 393220
  0.7 65.9 %copy-start.1 = (bf16[256,256]{1,0:T(8,128)(2,1)S(1)}, bf16[256,256]{1,0:T(8,128)(2,1)}, u32[]{:S(2)}) copy-start(bf16[256,256]{1,0:T(8,128)(2,1)} %constant.15.clone.rl_ref) | copy-start | bytes 393220
  0.7 65.9 %copy-start.2 = (bf16[256,256]{1,0:T(8,128)(2,1)S(1)}, bf16[256,256]{1,0:T(8,128)(2,1)}, u32[]{:S(2)}) copy-start(bf16[256,256]{1,0:T(8,128)(2,1)} %constant.16.clone.lh_ref) | copy-start | bytes 393220
  0.7 65.8 %copy-start.3 = (bf16[256,256]{1,0:T(8,128)(2,1)S(1)}, bf16[256,256]{1,0:T(8,128)(2,1)}, u32[]{:S(2)}) copy-start(bf16[256,256]{1,0:T(8,128)(2,1)} %constant.17.clone.ll_ref) | copy-start | bytes 393220

commit v2 on v1

v2 whole, which is shorter than its diff:
```python
import functools
import math

import jax
import jax.numpy as jnp
import numpy as np
from jax import lax
from jax.experimental import pallas as pl
from jax.experimental.pallas import tpu as pltpu
from jax.sharding import PartitionSpec as P

NG = 128
NZ = 8
NX = 4
FFT = 8
WIDE = NG // FFT
MESH = pl.DeviceIdType.MESH
SCALE = 0.25 * NG * math.sqrt(NG) / (NG * NG * NG)


def tables():
    index = np.arange(NG)
    angle = (index[:, None] * index[None, :] % NG) * (2.0 * np.pi / NG)
    high = np.stack([np.cos(angle), np.sin(angle)]).astype(jnp.bfloat16)
    low = (np.stack([np.cos(angle), np.sin(angle)]) - high.astype(np.float64)).astype(jnp.bfloat16)
    return np.stack([high, low])


def split(value):
    high = value.astype(jnp.bfloat16)
    low = (value - high.astype(jnp.float32)).astype(jnp.bfloat16)
    return high, low


def dot(a, b):
    return jnp.dot(a, b, preferred_element_type=jnp.float32)


def on_right(value, high, low):
    vh, vl = split(value)
    return dot(vh, high) + (dot(vl, high) + dot(vh, low))


def on_left(high, low, value):
    vh, vl = split(value)
    return dot(high, vh) + (dot(high, vl) + dot(low, vh))


def stack(parts):
    return jnp.concatenate([jnp.concatenate(p, axis=0) for p in parts], axis=1)


def unstack(value):
    return jnp.concatenate(
        [
            jnp.concatenate([value[:NG, s], value[NG:, s]], axis=1)
            for s in (slice(0, NG), slice(NG, 2 * NG))
        ],
        axis=0,
    )


HALF = NG // 2
SIDE = WIDE // 2
PAIRS = WIDE // 2


def each_shift(body):
    def step(i, carry):
        body(lax.rem(3 * i, FFT))
        return carry

    lax.fori_loop(1, FFT, step, 0)


def exchange(send_ref, recv_ref, start, count, half, send_sem, recv_sem, me):
    high, low = me // NX, lax.rem(me, NX)

    def body(k):
        there = lax.rem(high + k // NX, 2) * NX + lax.rem(low + k, NX)
        pltpu.make_async_remote_copy(
            send_ref.at[pl.ds(start, count), :, pl.ds(there * WIDE + half * SIDE, SIDE)],
            recv_ref.at[pl.ds(me * WIDE + start, count), :, pl.ds(half * SIDE, SIDE)],
            send_sem,
            recv_sem.at[half],
            device_id={"fft": there},
            device_id_type=MESH,
        ).start()

    each_shift(body)


def keep(send_ref, recv_ref, start, me):
    for p in (0, 1):
        recv_ref[me * WIDE + start + p] = send_ref[start + p, :, pl.ds(me * WIDE, WIDE)]


def arrived(recv_ref, half, sem):
    block = recv_ref.at[pl.ds(0, NG - WIDE), :, pl.ds(half * SIDE, SIDE)]
    pltpu.make_async_copy(block, block, sem.at[half]).wait()


def left(recv_ref, sem):
    block = recv_ref.at[pl.ds(0, NG - WIDE)]
    pltpu.make_async_copy(block, block, sem).wait()


def lines(recv_ref, row):
    flat = recv_ref.reshape(NG * 2 * WIDE, NG)
    return [flat[pl.ds(part * WIDE + row, NG, stride=2 * WIDE), :] for part in (0, 1)]


def field_kernel(
    root, pick_ref, core_ref, table_ref, x_ref, o_ref,
    r_ref, l_ref, s_ref, cand, send1, recv1, send2, recv2,
    ring_recv, pair_recv, cand_recv, ring_send, own_send, ss1, rs1, ss2, rs2,
):
    y0, z0 = root // NZ, root % NZ
    me = lax.axis_index("fft")
    band = lax.axis_index("band")
    y, z, c = band // 16, lax.rem(band // 2, NZ), lax.rem(band, 2)
    up, down = lax.rem(z + 1, NZ), lax.rem(z + NZ - 1, NZ)

    def at(yy, zz, cc):
        return {"band": yy * 16 + zz * 2 + cc}

    barrier = pltpu.get_barrier_semaphore()
    greet = [at(y, up, c), at(y, down, c), at(1 - y, z, c), at(y, z, 1 - c)]
    for device in greet:
        pl.semaphore_signal(barrier, inc=1, device_id=device, device_id_type=MESH)

    def greets(k):
        there = {"fft": lax.rem(me + k, FFT)}
        pl.semaphore_signal(barrier, inc=1, device_id=there, device_id_type=MESH)

    each_shift(greets)
    pl.semaphore_wait(barrier, len(greet) + FFT - 1)

    ahead = lax.rem(z - z0 + NZ, NZ)
    home = y == y0
    at_root = jnp.logical_and(home, ahead == 0)
    def remote(src, dst, send_sem, recv_sem, device):
        return pltpu.make_async_remote_copy(
            src, dst, send_sem, recv_sem, device_id=device, device_id_type=MESH
        )

    def waits(ref, sem):
        pltpu.make_async_copy(ref, ref, sem).wait()

    def pass_on(i, source=False):
        entry = jnp.where(i < 2, 1, jnp.where(i < 4, NZ - 1, 0))
        away = jnp.where(home, ahead, lax.rem(ahead - entry + NZ, NZ))
        goes = (
            (away < 4, at(y, up, c)),
            (jnp.logical_or(away == 0, away > 5), at(y, down, c)),
            (jnp.logical_and(home, ahead == entry), at(1 - y, z, c)),
        )
        if source:
            both = cand.at[pl.ds(2 * i, 2)]
            waits(both, cand_recv.at[i])
        for p in (0, 1):
            plane = 2 * i + p
            if source:
                s_ref[c, plane] = jnp.where(core_ref[0] == c, x_ref[c, plane], cand[plane])
            for half in (0, 1):
                here = s_ref.at[c, plane, pl.ds(half * HALF, HALF)]
                sem = ring_recv.at[2 * plane + half]
                if not source:
                    waits(here, sem)
                for way, (condition, device) in enumerate(goes):

                    @pl.when(condition)
                    def _():
                        remote(here, here, ring_send.at[way], sem, device).start()

        here = s_ref.at[c, pl.ds(2 * i, 2)]
        remote(here, here, own_send.at[0], pair_recv.at[i], at(y, z, 1 - c)).start()

    @pl.when(at_root)
    def _():
        def give(i, carry):
            both = pl.ds(2 * i, 2)
            remote(x_ref.at[1 - c, both], cand.at[both], own_send.at[1], cand_recv.at[i], at(y, z, 1 - c)).start()
            return carry

        lax.fori_loop(0, PAIRS, give, 0)

        def source(i, carry):
            pass_on(i, True)
            return carry

        lax.fori_loop(0, PAIRS, source, 0)

    def fill(n, carry):
        cosine, sine = table_ref[n, 0], table_ref[n, 1]
        for ref, near, far in ((r_ref, sine, -sine), (l_ref, -sine, sine)):
            ref[n, :NG, :NG] = cosine
            ref[n, NG:, NG:] = cosine
            ref[n, NG:, :NG] = near
            ref[n, :NG, NG:] = far
        return carry

    lax.fori_loop(0, 2, fill, 0)

    @pl.when(at_root)
    def _():
        crossed = s_ref.at[0, pl.ds(0, 8)]
        waits(crossed, ring_send.at[2])

    pick = pick_ref[0, 0]

    def forward(i):
        start = 2 * i
        rows = []
        waits(s_ref.at[0, pl.ds(0, 2)], pair_recv.at[i])
        for p in (0, 1):
            chosen = x_ref[pick, start + p]
            rows.append(jnp.concatenate([s_ref[0, start + p] * chosen, s_ref[1, start + p] * chosen], axis=1))
        value = on_right(jnp.concatenate(rows, axis=0), r_ref[0], r_ref[1])
        value = stack([[value[p * NG:(p + 1) * NG, :NG], value[p * NG:(p + 1) * NG, NG:]] for p in (0, 1)])
        value = on_left(l_ref[0], l_ref[1], value)
        for p in (0, 1):
            for part in (0, 1):
                send1[start + p, part] = value[part * NG:(part + 1) * NG, p * NG:(p + 1) * NG]
        for half in (0, 1):
            exchange(send1, recv1, start, 2, half, ss1, rs1, me)
        keep(send1, recv1, start, me)

    lag = jnp.where(jnp.logical_and(home, ahead == 1), 3, jnp.where(jnp.logical_and(home, ahead == NZ - 1), 4, 1))

    def stream(i, carry):
        @pl.when(jnp.logical_and(i < PAIRS, jnp.logical_not(at_root)))
        def _():
            pass_on(i)

        @pl.when(jnp.logical_and(i >= lag, i < lag + PAIRS))
        def _():
            forward(i - lag)

        return carry

    lax.fori_loop(0, PAIRS + 4, stream, 0)

    first = lax.broadcasted_iota(jnp.int32, (NG, NG), 0)
    last = lax.broadcasted_iota(jnp.int32, (NG, NG), 1)
    signed = lambda n: jnp.where(n < NG // 2, n, n - NG)
    first, last = signed(first), signed(last)
    flat = first * first + last * last

    def middle(i, carry):
        for half in (0, 1):

            @pl.when(i == half * (PAIRS // 2))
            def _():
                arrived(recv1, half, rs1)

        start = 2 * i
        value = stack([lines(recv1, start + p) for p in (0, 1)])
        value = on_left(l_ref[0], l_ref[1], value)
        filters = []
        for p in (0, 1):
            second = me * WIDE + start + p
            second = second - NG * (second // (NG // 2))
            square = flat + second * second
            ratio = SCALE / jnp.maximum(square, 1).astype(jnp.float32)
            filters.append(jnp.where(square > 0, ratio, 0.0))
        filters = jnp.concatenate(filters, axis=1)
        value = jnp.concatenate([value[:NG] * filters, value[NG:] * filters], axis=0)
        value = on_left(r_ref[0], r_ref[1], value)
        for p in (0, 1):
            for part in (0, 1):
                send2[start + p, part] = value[part * NG:(part + 1) * NG, p * NG:(p + 1) * NG]
        exchange(send2, recv2, start, 2, 0, ss2, rs2, me)
        keep(send2, recv2, start, me)
        return carry

    lax.fori_loop(0, PAIRS, middle, 0)
    exchange(send2, recv2, 0, WIDE, 1, ss2, rs2, me)

    def backward(i, carry):
        for half in (0, 1):

            @pl.when(i == half * (PAIRS // 2))
            def _():
                arrived(recv2, half, rs2)

        start = 2 * i
        value = stack([lines(recv2, start + p) for p in (0, 1)])
        value = on_left(r_ref[0], r_ref[1], value)
        value = on_right(unstack(value), l_ref[0], l_ref[1])
        for p in (0, 1):
            part = value[p * NG:(p + 1) * NG]
            o_ref[start + p] = part[:, :NG] * s_ref[0, start + p] + part[:, NG:] * s_ref[1, start + p]
        return carry

    lax.fori_loop(0, PAIRS, backward, 0)

    whole, half_of, quarter = s_ref.at[0], s_ref.at[0, pl.ds(0, 8)], s_ref.at[0, pl.ds(0, 4)]
    for way in (0, 1):
        for first_entry, block in ((0, half_of), (1, quarter), (NZ - 1, quarter)):
            away = jnp.where(home, ahead, lax.rem(ahead - first_entry + NZ, NZ))
            went = away < 4 if way == 0 else jnp.logical_or(away == 0, away > 5)

            @pl.when(went)
            def _():
                waits(block, ring_send.at[way])

    @pl.when(jnp.logical_and(home, jnp.logical_or(ahead == 1, ahead == NZ - 1)))
    def _():
        waits(quarter, ring_send.at[2])

    waits(whole, own_send.at[0])

    @pl.when(at_root)
    def _():
        waits(whole, own_send.at[1])

    left(recv1, ss1)
    left(recv2, ss2)


def field(root, pick, core, orbitals, table):
    vmem = pl.BlockSpec(memory_space=pltpu.VMEM)
    smem = pl.BlockSpec(memory_space=pltpu.SMEM)
    dma = pltpu.SemaphoreType.DMA
    shapes = [(2, WIDE, NG, NG), (WIDE, NG, NG)]
    shapes += [(WIDE, 2, NG, NG), (NG, 2, WIDE, NG)] * 2
    sems = [(2 * WIDE,), (PAIRS,), (PAIRS,), (3,), (2,), (), (2,), (), (2,)]
    return pl.pallas_call(
        functools.partial(field_kernel, root),
        out_shape=jax.ShapeDtypeStruct(orbitals.shape[1:], orbitals.dtype),
        in_specs=[smem] * 2 + [vmem] * 2,
        out_specs=vmem,
        scratch_shapes=[pltpu.VMEM((2, 2 * NG, 2 * NG), jnp.bfloat16)] * 2
        + [pltpu.VMEM(shape, jnp.float32) for shape in shapes]
        + [dma(shape) for shape in sems],
        compiler_params=pltpu.CompilerParams(collective_id=root, has_side_effects=True, vmem_limit_bytes=48 << 20),
        name=f"field_{root}",
    )(pick, core, table, orbitals)


def on_device(orbitals, owners, local_pick):
    table = lax.optimization_barrier(jnp.asarray(tables()))
    branches = [functools.partial(field, root) for root in range(2 * NZ)]
    return lax.switch(owners[0] // 2, branches, local_pick, owners % 2, orbitals, table)[None]


def solution(mesh):
    in_specs = (P("band", "fft", None, None), P(), P("band", None))
    out_specs = P("band", "fft", None, None)
    return jax.shard_map(on_device, mesh=mesh, in_specs=in_specs, out_specs=out_specs, check_vma=False)
```

time: 134 us -> 98.9 us (0.74); the launches traced: 134 us -> 97.1 us
  Pallas kernels: 131 us -> 94.6 us
    pallas_call x2 -> x1, Pallas kernels: 131 us -> 94.6 us  [field(): pl.pallas_call(functools.partial(field_kernel, root), out_shape=jax.Shape...]
where the time goes in v2:
time: 98.9 us; the launch traced here: 97.1 us
  Pallas kernels  94.6 us (96%)
    pallas_call x1, Pallas kernels, field(): pl.pallas_call(functools.partial(field_kernel, root), out_shape=jax.Shape...  94.6 us

profile of v2, /device:TPU:1, one launch (start us, length us, event | category | flops | bytes accessed | tf_op | source)
XLA Modules:
  0.0 97.1 jit_solution(7245677659235438243)
XLA Ops:
  0.7 95.4 %conditional.1 = (f32[1,16,128,128]{3,2,1,0:T(8,128)S(1)}) conditional(s32[]{:T(128)} %clamp.3, (s32[1,1]{1,0:T(1,128)}, s32[1]{0:T(128)}, bf16[2,2,128,128]{3,2,1,0:T(8,128)(2,1)}, f32[2,16,128,128]{3,2,1,0:T(8,128)}, s32[1]{0:T(128)}, /*index=5*/s32[1]{0:T(128)}, s32[1]{0:T(128)}, s32[1]{0:T(128)}) %tuple.88, ...), branch_computations={%region_0.1_spmd.clone, %region_1.2_spmd.clone, %region_2.3_spmd.c... | conditional | flops 5 | bytes 54 | solution.py:345
  1.2 94.6 %field_14.1 = f32[16,128,128]{2,1,0:T(8,128)S(1)} custom-call(s32[1,1]{1,0:T(1,128)} %get-tuple-element.696.pick_ref, s32[1]{0:T(128)S(6)} %select_n.43.core_ref, bf16[2,2,128,128]{3,2,1,0:T(8,128)(2,1)} %get-tuple-element.694.table_ref, f32[2,16,128,128]{3,2,1,0:T(8,128)} %get-tuple-element.698.x_ref), custom_call_target="tpu_custom_call" | custom-call | tf_op jit(solution)/shard_map/cond/branch_14_fun/field_14/pallas_call | solution.py:329
  96.1 1.0 %copy.119 = f32[1,16,128,128]{3,2,1,0:T(8,128)} copy(f32[1,16,128,128]{3,2,1,0:T(8,128)S(1)} %get-tuple-element.215) | data formatting | bytes 2097152

commit v3 on v2

--- a/solution.py
+++ b/solution.py
@@ -111,9 +111,9 @@
 
 
 def field_kernel(
-    root, pick_ref, core_ref, table_ref, x_ref, o_ref,
-    r_ref, l_ref, s_ref, cand, send1, recv1, send2, recv2,
-    ring_recv, pair_recv, cand_recv, ring_send, own_send, ss1, rs1, ss2, rs2,
+    root, pick_ref, core_ref, table_hbm, x_hbm, o_hbm,
+    table_ref, x_ref, o_ref, r_ref, l_ref, s_ref, cand, send1, recv1, send2, recv2,
+    ring_recv, pair_recv, cand_recv, ring_send, own_send, ss1, rs1, ss2, rs2, own_copy,
 ):
     y0, z0 = root // NZ, root % NZ
     me = lax.axis_index("fft")
@@ -124,6 +124,10 @@
     def at(yy, zz, cc):
         return {"band": yy * 16 + zz * 2 + cc}
 
+    x_copy = pltpu.make_async_copy(x_hbm, x_ref, own_copy.at[0])
+    table_copy = pltpu.make_async_copy(table_hbm, table_ref, own_copy.at[1])
+    x_copy.start()
+    table_copy.start()
     barrier = pltpu.get_barrier_semaphore()
     greet = [at(y, up, c), at(y, down, c), at(1 - y, z, c), at(y, z, 1 - c)]
     for device in greet:
@@ -134,6 +138,7 @@
         pl.semaphore_signal(barrier, inc=1, device_id=there, device_id_type=MESH)
 
     each_shift(greets)
+    x_copy.wait()
     pl.semaphore_wait(barrier, len(greet) + FFT - 1)
 
     ahead = lax.rem(z - z0 + NZ, NZ)
@@ -147,49 +152,82 @@
     def waits(ref, sem):
         pltpu.make_async_copy(ref, ref, sem).wait()
 
-    def pass_on(i, source=False):
-        entry = jnp.where(i < 2, 1, jnp.where(i < 4, NZ - 1, 0))
+    def ship(pair, q, way):
+        here = s_ref.at[c, 2 * pair + q // 2, pl.ds(lax.rem(q, 2) * HALF, HALF)]
+        ring = y * 16 + jnp.where(way == 0, up, down) * 2 + c
+        device = {"band": jnp.where(way == 2, (1 - y) * 16 + z * 2 + c, ring)}
+        remote(here, here, ring_send.at[way], ring_recv.at[4 * pair + q], device).start()
+
+    def share(pair):
+        here = s_ref.at[c, pl.ds(2 * pair, 2)]
+        remote(here, here, own_send.at[0], pair_recv.at[pair], at(y, z, 1 - c)).start()
+
+    def repeat(start, stop, body):
+        def step(i, carry):
+            body(i)
+            return carry
+
+        lax.fori_loop(start, stop, step, 0)
+
+    def pass_on(pair):
+        entry = jnp.where(pair < 2, 1, jnp.where(pair < 4, NZ - 1, 0))
         away = jnp.where(home, ahead, lax.rem(ahead - entry + NZ, NZ))
         goes = (
-            (away < 4, at(y, up, c)),
-            (jnp.logical_or(away == 0, away > 5), at(y, down, c)),
-            (jnp.logical_and(home, ahead == entry), at(1 - y, z, c)),
+            away < 4,
+            jnp.logical_or(away == 0, away > 5),
+            jnp.logical_and(home, ahead == entry),
         )
-        if source:
-            both = cand.at[pl.ds(2 * i, 2)]
-            waits(both, cand_recv.at[i])
-        for p in (0, 1):
-            plane = 2 * i + p
-            if source:
-                s_ref[c, plane] = jnp.where(core_ref[0] == c, x_ref[c, plane], cand[plane])
-            for half in (0, 1):
-                here = s_ref.at[c, plane, pl.ds(half * HALF, HALF)]
-                sem = ring_recv.at[2 * plane + half]
-                if not source:
-                    waits(here, sem)
-                for way, (condition, device) in enumerate(goes):
-
-                    @pl.when(condition)
-                    def _():
-                        remote(here, here, ring_send.at[way], sem, device).start()
-
-        here = s_ref.at[c, pl.ds(2 * i, 2)]
-        remote(here, here, own_send.at[0], pair_recv.at[i], at(y, z, 1 - c)).start()
+
+        def quarter(q):
+            here = s_ref.at[c, 2 * pair + q // 2, pl.ds(lax.rem(q, 2) * HALF, HALF)]
+            waits(here, ring_recv.at[4 * pair + q])
+            for way, condition in enumerate(goes):
+
+                @pl.when(condition)
+                def _():
+                    ship(pair, q, way)
+
+        repeat(0, 4, quarter)
+        share(pair)
+
+    def turned(i):
+        return jnp.where(i < 4, lax.rem(i + 2, 4), i)
+
+    def order(i):
+        near = jnp.where(ahead > 4, turned(i), i)
+        k = lax.rem(i + 4, PAIRS)
+        far = jnp.where(ahead > 4, turned(k), k)
+        swapped = jnp.logical_and(ahead == 0, jnp.logical_or(k == 1, k == 2))
+        return jnp.where(home, near, jnp.where(swapped, 3 - k, far))
 
     @pl.when(at_root)
     def _():
-        def give(i, carry):
-            both = pl.ds(2 * i, 2)
-            remote(x_ref.at[1 - c, both], cand.at[both], own_send.at[1], cand_recv.at[i], at(y, z, 1 - c)).start()
-            return carry
-
-        lax.fori_loop(0, PAIRS, give, 0)
-
-        def source(i, carry):
-            pass_on(i, True)
-            return carry
-
-        lax.fori_loop(0, PAIRS, source, 0)
+        def nth(j):
+            return jnp.where(j < 6, 2 * lax.rem(j, 3) + j // 3, j)
+
+        def give(j):
+            both = pl.ds(2 * nth(j), 2)
+            remote(x_ref.at[1 - c, both], cand.at[both], own_send.at[1], cand_recv.at[nth(j)], at(y, z, 1 - c)).start()
+
+        repeat(0, PAIRS, give)
+
+        def source(j):
+            pair = nth(j)
+            waits(cand.at[pl.ds(0, 2)], cand_recv.at[pair])
+            for p in (0, 1):
+                plane = 2 * pair + p
+                s_ref[c, plane] = jnp.where(core_ref[0] == c, x_ref[c, plane], cand[plane])
+            repeat(0, 4, lambda q: ship(pair, q, jnp.where(j < 6, lax.rem(j, 3), 2)))
+            share(pair)
+
+        repeat(0, PAIRS, source)
+
+        def rest(i):
+            repeat(0, 8, lambda q: ship(jnp.where(q < 4, i, turned(i)), lax.rem(q, 4), q // 4))
+
+        repeat(2, PAIRS, rest)
+
+    table_copy.wait()
 
     def fill(n, carry):
         cosine, sine = table_ref[n, 0], table_ref[n, 1]
@@ -210,9 +248,10 @@
     pick = pick_ref[0, 0]
 
     def forward(i):
-        start = 2 * i
+        pair = order(i)
+        start = 2 * pair
         rows = []
-        waits(s_ref.at[0, pl.ds(0, 2)], pair_recv.at[i])
+        waits(s_ref.at[0, pl.ds(0, 2)], pair_recv.at[pair])
         for p in (0, 1):
             chosen = x_ref[pick, start + p]
             rows.append(jnp.concatenate([s_ref[0, start + p] * chosen, s_ref[1, start + p] * chosen], axis=1))
@@ -226,12 +265,12 @@
             exchange(send1, recv1, start, 2, half, ss1, rs1, me)
         keep(send1, recv1, start, me)
 
-    lag = jnp.where(jnp.logical_and(home, ahead == 1), 3, jnp.where(jnp.logical_and(home, ahead == NZ - 1), 4, 1))
+    lag = jnp.where(jnp.logical_and(home, jnp.logical_or(ahead == 1, ahead == NZ - 1)), 3, 1)
 
     def stream(i, carry):
         @pl.when(jnp.logical_and(i < PAIRS, jnp.logical_not(at_root)))
         def _():
-            pass_on(i)
+            pass_on(order(i))
 
         @pl.when(jnp.logical_and(i >= lag, i < lag + PAIRS))
         def _():
@@ -239,7 +278,7 @@
 
         return carry
 
-    lax.fori_loop(0, PAIRS + 4, stream, 0)
+    lax.fori_loop(0, PAIRS + 3, stream, 0)
 
     first = lax.broadcasted_iota(jnp.int32, (NG, NG), 0)
     last = lax.broadcasted_iota(jnp.int32, (NG, NG), 1)
@@ -291,6 +330,8 @@
         for p in (0, 1):
             part = value[p * NG:(p + 1) * NG]
             o_ref[start + p] = part[:, :NG] * s_ref[0, start + p] + part[:, NG:] * s_ref[1, start + p]
+        both = pl.ds(start, 2)
+        pltpu.make_async_copy(o_ref.at[both], o_hbm.at[both], own_copy.at[2]).start()
         return carry
 
     lax.fori_loop(0, PAIRS, backward, 0)
@@ -315,23 +356,25 @@
     def _():
         waits(whole, own_send.at[1])
 
+    pltpu.make_async_copy(o_ref, o_hbm, own_copy.at[2]).wait()
     left(recv1, ss1)
     left(recv2, ss2)
 
 
 def field(root, pick, core, orbitals, table):
-    vmem = pl.BlockSpec(memory_space=pltpu.VMEM)
     smem = pl.BlockSpec(memory_space=pltpu.SMEM)
+    place = pl.BlockSpec(memory_space=pl.ANY)
     dma = pltpu.SemaphoreType.DMA
     shapes = [(2, WIDE, NG, NG), (WIDE, NG, NG)]
     shapes += [(WIDE, 2, NG, NG), (NG, 2, WIDE, NG)] * 2
-    sems = [(2 * WIDE,), (PAIRS,), (PAIRS,), (3,), (2,), (), (2,), (), (2,)]
+    sems = [(2 * WIDE,), (PAIRS,), (PAIRS,), (3,), (2,), (), (2,), (), (2,), (3,)]
     return pl.pallas_call(
         functools.partial(field_kernel, root),
         out_shape=jax.ShapeDtypeStruct(orbitals.shape[1:], orbitals.dtype),
-        in_specs=[smem] * 2 + [vmem] * 2,
-        out_specs=vmem,
-        scratch_shapes=[pltpu.VMEM((2, 2 * NG, 2 * NG), jnp.bfloat16)] * 2
+        in_specs=[smem] * 2 + [place] * 2,
+        out_specs=place,
+        scratch_shapes=[pltpu.VMEM(table.shape, table.dtype), pltpu.VMEM(orbitals.shape, jnp.float32), pltpu.VMEM(orbitals.shape[1:], jnp.float32)]
+        + [pltpu.VMEM((2, 2 * NG, 2 * NG), jnp.bfloat16)] * 2
         + [pltpu.VMEM(shape, jnp.float32) for shape in shapes]
         + [dma(shape) for shape in sems],
         compiler_params=pltpu.CompilerParams(collective_id=root, has_side_effects=True, vmem_limit_bytes=48 << 20),

time: 98.9 us -> 87.8 us (0.89); the launches traced: 97.1 us -> 87.5 us
  Pallas kernels: 94.6 us -> 85.1 us
    pallas_call x1, Pallas kernels: 94.6 us -> 85.1 us  [field(): pl.pallas_call(functools.partial(field_kernel, root), out_shape=jax.Shape...]
where the time goes in v3:
time: 87.8 us; the launch traced here: 87.5 us
  Pallas kernels  85.1 us (97%)
  local copies, waits for them, and re-layouts  0.97 us (1%)
    pallas_call x1, Pallas kernels, field(): pl.pallas_call(functools.partial(field_kernel, root), out_shape=jax.Shape...  85.1 us

profile of v3, /device:TPU:1, one launch (start us, length us, event | category | flops | bytes accessed | tf_op | source)
XLA Modules:
  0.0 87.5 jit_solution(10602414931976951240)
XLA Ops:
  0.7 85.8 %conditional.1 = (f32[1,16,128,128]{3,2,1,0:T(8,128)S(1)}) conditional(s32[]{:T(128)} %clamp.3, (s32[1,1]{1,0:T(1,128)}, s32[1]{0:T(128)}, bf16[2,2,128,128]{3,2,1,0:T(8,128)(2,1)}, f32[2,16,128,128]{3,2,1,0:T(8,128)}, s32[1]{0:T(128)}, /*index=5*/s32[1]{0:T(128)}, s32[1]{0:T(128)}, s32[1]{0:T(128)}) %tuple.88, ...), branch_computations={%region_0.1_spmd.clone, %region_1.2_spmd.clone, %region_2.3_spmd.c... | conditional | flops 5 | bytes 54 | solution.py:388
  0.7 85.1 %field_4.1 = f32[16,128,128]{2,1,0:T(8,128)S(1)} custom-call(s32[1,1]{1,0:T(1,128)} %get-tuple-element.526.pick_ref, s32[1]{0:T(128)S(6)} %select_n.33.core_ref, bf16[2,2,128,128]{3,2,1,0:T(8,128)(2,1)} %get-tuple-element.524.table_hbm, f32[2,16,128,128]{3,2,1,0:T(8,128)} %get-tuple-element.528.x_hbm), custom_call_target="tpu_custom_call" | custom-call | tf_op jit(solution)/shard_map/cond/branch_4_fun/field_4/pallas_call | solution.py:371
  86.5 1.0 %copy.119 = f32[1,16,128,128]{3,2,1,0:T(8,128)} copy(f32[1,16,128,128]{3,2,1,0:T(8,128)S(1)} %get-tuple-element.215) | data formatting | bytes 2097152
